TPU v7x, 32 devices: a whole 2x2x4 slice. The times are simulated.
32 devices in a mesh: fsdp: 32 (over z, y, x, core).
Axes of the slice: x: 2, y: 2, z: 4, core: 2. Of those that a mesh axis runs over, the one named last changes fastest.
Arguments:
- block_input: bfloat16 [32, 784, 768], P('fsdp'), may hold values from -6 to 6
- seg_ids: int32 [32, 784], P('fsdp'), may hold values from 0 to 3, as said below
- gain_attn: bfloat16 [768], P('fsdp'), may hold values from 0.099609375 to 1.8984375
- w_query: bfloat16 [768, 768], P('fsdp'), may hold values from -0.21875 to 0.21875
- w_key: bfloat16 [768, 768], P('fsdp'), may hold values from -0.21875 to 0.21875
- w_value: bfloat16 [768, 768], P('fsdp'), may hold values from -0.21875 to 0.21875
- w_out: bfloat16 [768, 768], P('fsdp'), may hold values from -0.875 to 0.875
- gain_ffn: bfloat16 [768], P('fsdp'), may hold values from 0.099609375 to 1.8984375
- w_gate: bfloat16 [768, 2048], P('fsdp'), may hold values from -0.21875 to 0.21875
- w_up: bfloat16 [768, 2048], P('fsdp'), may hold values from -0.21875 to 0.21875
- w_down: bfloat16 [2048, 768], P('fsdp'), may hold values from -0.125 to 0.125
- cotangent: bfloat16 [32, 784, 768], P('fsdp'), may hold values from -6 to 6
Outputs:
- block_output: bfloat16 [32, 784, 768], P('fsdp')
- input_grad: bfloat16 [32, 784, 768], P('fsdp')
- gain_attn_grad: float32 [768], P('fsdp')
- w_query_grad: float32 [768, 768], P('fsdp')
- w_key_grad: float32 [768, 768], P('fsdp')
- w_value_grad: float32 [768, 768], P('fsdp')
- w_out_grad: float32 [768, 768], P('fsdp')
- gain_ffn_grad: float32 [768], P('fsdp')
- w_gate_grad: float32 [768, 2048], P('fsdp')
- w_up_grad: float32 [768, 2048], P('fsdp')
- w_down_grad: float32 [2048, 768], P('fsdp')
Inputs may be any that keep to these rules, and one draw needn't show every extreme that they name: `seg_ids`: each row holds, from slot 0 on, either one image of 577 tokens (segment 0) or two or three images of 257 tokens (segments 0, 1, 2 in order), and padding with segment number 3 in all remaining slots, at least one of them.
All inputs are finite; a program needn't handle non-finite values.
Results may differ from a plain program's by a relative error of at most 0.015.
Values may be sent and summed in bfloat16 or wider, within the bound.
A program may use at most 128 MiB of HBM per device.

v0:
```python
from functools import partial
import jax
import jax.numpy as jnp
from jax import lax
from jax.sharding import PartitionSpec as P

HEAD = 64
EPSILON = 1e-05


def rope_tables(segment_row, head_size):
    length = segment_row.shape[0]
    places = jnp.arange(length, dtype=jnp.int32)
    labels = jnp.arange(4, dtype=jnp.int32)
    counts = jnp.sum((segment_row[:, None] == labels[None, :]).astype(jnp.int32), axis=0)
    before = (labels[None, :] < segment_row[:, None]).astype(jnp.int32)
    starts = jnp.sum(before * counts[None, :], axis=1)
    offsets = (places - starts).astype(jnp.float32)
    frequency = 10000.0 ** (-(jnp.arange(head_size // 2, dtype=jnp.float32) * 2.0) / head_size)
    angles = offsets[:, None] * frequency[None, :]
    return (jnp.cos(angles), jnp.sin(angles))


def rotate(values, cosine, sine_table):
    half_size = values.shape[-1] // 2
    lower_half = values[..., :half_size]
    upper_half = values[..., half_size:]
    cosine = cosine[..., None, :]
    sine_table = sine_table[..., None, :]
    return jnp.concatenate(
        [
            lower_half * cosine - upper_half * sine_table,
            upper_half * cosine + lower_half * sine_table,
        ],
        axis=-1,
    )


def unrotate(gradient, cosine, sine_table):
    half_size = gradient.shape[-1] // 2
    lower_half = gradient[..., :half_size]
    upper_half = gradient[..., half_size:]
    cosine = cosine[..., None, :]
    sine_table = sine_table[..., None, :]
    return jnp.concatenate(
        [
            lower_half * cosine + upper_half * sine_table,
            upper_half * cosine - lower_half * sine_table,
        ],
        axis=-1,
    )


def head_forward(query_head, key_head, value_head, allowed, score_scale):
    raw_scores = jnp.einsum("le,me->lm", query_head, key_head, preferred_element_type=jnp.float32)
    masked = jnp.where(allowed, raw_scores * score_scale, -1e30)
    highest = jnp.max(masked, axis=-1, keepdims=True)
    exponent = jnp.exp(masked - highest)
    denominator = jnp.sum(exponent, axis=-1, keepdims=True)
    weights = (exponent / denominator).astype(jnp.bfloat16)
    mixture = jnp.dot(weights, value_head, preferred_element_type=jnp.float32)
    return (mixture, (highest + jnp.log(denominator))[:, 0])


def head_backward(query_head, key_head, value_head, grad_head, logsum, allowed, score_scale):
    raw_scores = jnp.einsum("le,me->lm", query_head, key_head, preferred_element_type=jnp.float32)
    masked = jnp.where(allowed, raw_scores * score_scale, -1e30)
    probabilities = jnp.exp(masked - logsum[:, None])
    weights = probabilities.astype(jnp.bfloat16)
    grad_value = jnp.einsum("lm,le->me", weights, grad_head, preferred_element_type=jnp.float32)
    grad_probs = jnp.einsum("le,me->lm", grad_head, value_head, preferred_element_type=jnp.float32)
    grad_scores = probabilities * (
        grad_probs - jnp.sum(grad_probs * probabilities, axis=-1, keepdims=True)
    )
    grad_scores = grad_scores.astype(jnp.bfloat16)
    grad_query = jnp.dot(grad_scores, key_head, preferred_element_type=jnp.float32) * score_scale
    grad_key = (
        jnp.einsum("lm,le->me", grad_scores, query_head, preferred_element_type=jnp.float32)
        * score_scale
    )
    return (grad_query, grad_key, grad_value)


def norm_backward(grad_normed, normed, inverse, gain):
    scaled = grad_normed * gain
    return inverse * (scaled - normed * jnp.mean(scaled * normed, axis=-1, keepdims=True))


def per_device(
    block_input,
    seg_ids,
    gain_attn,
    w_query,
    w_key,
    w_value,
    w_out,
    gain_ffn,
    w_gate,
    w_up,
    w_down,
    cotangent,
):
    row_count, length, width = block_input.shape
    head_count = width // HEAD
    tokens = row_count * length
    score_scale = HEAD ** (-0.5)
    attn_set = (
        lax.all_gather(gain_attn, "fsdp", axis=0, tiled=True),
        lax.all_gather(w_query, "fsdp", axis=0, tiled=True),
        lax.all_gather(w_key, "fsdp", axis=0, tiled=True),
        lax.all_gather(w_value, "fsdp", axis=0, tiled=True),
        lax.all_gather(w_out, "fsdp", axis=0, tiled=True),
    )
    ffn_set = (
        lax.all_gather(gain_ffn, "fsdp", axis=0, tiled=True),
        lax.all_gather(w_gate, "fsdp", axis=0, tiled=True),
        lax.all_gather(w_up, "fsdp", axis=0, tiled=True),
        lax.all_gather(w_down, "fsdp", axis=0, tiled=True),
    )
    cosine, sine_table = jax.vmap(partial(rope_tables, head_size=HEAD))(seg_ids)
    places = jnp.arange(length, dtype=jnp.int32)
    allowed = (seg_ids[:, :, None] == seg_ids[:, None, :]) & (
        places[None, None, :] <= places[None, :, None]
    )
    inputs = block_input.reshape(tokens, width).astype(jnp.float32)
    scale_one = lax.rsqrt(jnp.mean(inputs * inputs, axis=-1, keepdims=True) + EPSILON)
    normed_one = inputs * scale_one
    normed_low = (normed_one * attn_set[0].astype(jnp.float32)).astype(jnp.bfloat16)
    queries = jnp.dot(normed_low, attn_set[1], preferred_element_type=jnp.float32).reshape(
        row_count, length, head_count, HEAD
    )
    key_vectors = jnp.dot(normed_low, attn_set[2], preferred_element_type=jnp.float32).reshape(
        row_count, length, head_count, HEAD
    )
    value_vectors = jnp.dot(normed_low, attn_set[3], preferred_element_type=jnp.float32).astype(
        jnp.bfloat16
    )
    value_vectors = value_vectors.reshape(row_count, length, head_count, HEAD)
    query_rot = rotate(queries, cosine, sine_table).astype(jnp.bfloat16)
    key_rot = rotate(key_vectors, cosine, sine_table).astype(jnp.bfloat16)
    query_heads = jnp.moveaxis(query_rot, 2, 1)
    key_heads = jnp.moveaxis(key_rot, 2, 1)
    value_heads = jnp.moveaxis(value_vectors, 2, 1)

    def row_forward(operands):
        query_row, key_row, value_row, allowed_row = operands

        def one_head(head_parts):
            return head_forward(
                head_parts[0], head_parts[1], head_parts[2], allowed_row, score_scale
            )

        return lax.map(one_head, (query_row, key_row, value_row))

    mixture, logsum = lax.map(row_forward, (query_heads, key_heads, value_heads, allowed))
    attn_low = jnp.moveaxis(mixture, 1, 2).reshape(tokens, width).astype(jnp.bfloat16)
    middle = inputs + jnp.dot(attn_low, attn_set[4], preferred_element_type=jnp.float32)
    scale_two = lax.rsqrt(jnp.mean(middle * middle, axis=-1, keepdims=True) + EPSILON)
    normed_two = middle * scale_two
    ffn_low = (normed_two * ffn_set[0].astype(jnp.float32)).astype(jnp.bfloat16)
    gate_proj = jnp.dot(ffn_low, ffn_set[1], preferred_element_type=jnp.float32)
    up_proj = jnp.dot(ffn_low, ffn_set[2], preferred_element_type=jnp.float32)
    gate_sigm = jax.nn.sigmoid(gate_proj)
    activated = gate_proj * gate_sigm
    hidden = (activated * up_proj).astype(jnp.bfloat16)
    output_full = middle + jnp.dot(hidden, ffn_set[3], preferred_element_type=jnp.float32)
    output = output_full.astype(jnp.bfloat16).reshape(row_count, length, width)
    grad_out = cotangent.reshape(tokens, width).astype(jnp.float32)
    grad_low = grad_out.astype(jnp.bfloat16)
    down_grad = jnp.einsum("tf,td->fd", hidden, grad_low, preferred_element_type=jnp.float32)
    grad_hidden = jnp.einsum("td,fd->tf", grad_low, ffn_set[3], preferred_element_type=jnp.float32)
    gate_grad_low = (
        grad_hidden * up_proj * gate_sigm * (1.0 + gate_proj * (1.0 - gate_sigm))
    ).astype(jnp.bfloat16)
    up_grad_low = (grad_hidden * activated).astype(jnp.bfloat16)
    gate_grad = jnp.einsum("td,tf->df", ffn_low, gate_grad_low, preferred_element_type=jnp.float32)
    up_grad = jnp.einsum("td,tf->df", ffn_low, up_grad_low, preferred_element_type=jnp.float32)
    grad_normed_two = jnp.einsum(
        "tf,df->td", gate_grad_low, ffn_set[1], preferred_element_type=jnp.float32
    )
    grad_normed_two = grad_normed_two + jnp.einsum(
        "tf,df->td", up_grad_low, ffn_set[2], preferred_element_type=jnp.float32
    )
    gain_two_grad = jnp.sum(grad_normed_two * normed_two, axis=0)
    grad_middle = grad_out + norm_backward(
        grad_normed_two, normed_two, scale_two, ffn_set[0].astype(jnp.float32)
    )
    ffn_parts = (
        lax.psum_scatter(gain_two_grad, "fsdp", scatter_dimension=0, tiled=True),
        lax.psum_scatter(gate_grad, "fsdp", scatter_dimension=0, tiled=True),
        lax.psum_scatter(up_grad, "fsdp", scatter_dimension=0, tiled=True),
        lax.psum_scatter(down_grad, "fsdp", scatter_dimension=0, tiled=True),
    )
    branch_low = grad_middle.astype(jnp.bfloat16)
    out_grad = jnp.einsum("te,td->ed", attn_low, branch_low, preferred_element_type=jnp.float32)
    grad_attn = jnp.einsum(
        "td,ed->te", branch_low, attn_set[4], preferred_element_type=jnp.float32
    ).astype(jnp.bfloat16)
    grad_heads = jnp.moveaxis(grad_attn.reshape(row_count, length, head_count, HEAD), 2, 1)

    def row_backward(operands):
        query_row, key_row, value_row, grad_row, logsum_row, allowed_row = operands

        def one_head(head_parts):
            return head_backward(
                head_parts[0],
                head_parts[1],
                head_parts[2],
                head_parts[3],
                head_parts[4],
                allowed_row,
                score_scale,
            )

        return lax.map(one_head, (query_row, key_row, value_row, grad_row, logsum_row))

    grad_query_heads, grad_key_heads, grad_value_heads = lax.map(
        row_backward, (query_heads, key_heads, value_heads, grad_heads, logsum, allowed)
    )
    query_grad_low = (
        unrotate(jnp.moveaxis(grad_query_heads, 1, 2), cosine, sine_table)
        .reshape(tokens, width)
        .astype(jnp.bfloat16)
    )
    key_grad_low = (
        unrotate(jnp.moveaxis(grad_key_heads, 1, 2), cosine, sine_table)
        .reshape(tokens, width)
        .astype(jnp.bfloat16)
    )
    value_grad_low = (
        jnp.moveaxis(grad_value_heads, 1, 2).reshape(tokens, width).astype(jnp.bfloat16)
    )
    query_grad = jnp.einsum(
        "td,te->de", normed_low, query_grad_low, preferred_element_type=jnp.float32
    )
    key_grad = jnp.einsum("td,te->de", normed_low, key_grad_low, preferred_element_type=jnp.float32)
    value_grad = jnp.einsum(
        "td,te->de", normed_low, value_grad_low, preferred_element_type=jnp.float32
    )
    grad_normed_one = jnp.einsum(
        "te,de->td", query_grad_low, attn_set[1], preferred_element_type=jnp.float32
    )
    grad_normed_one = grad_normed_one + jnp.einsum(
        "te,de->td", key_grad_low, attn_set[2], preferred_element_type=jnp.float32
    )
    grad_normed_one = grad_normed_one + jnp.einsum(
        "te,de->td", value_grad_low, attn_set[3], preferred_element_type=jnp.float32
    )
    gain_one_grad = jnp.sum(grad_normed_one * normed_one, axis=0)
    input_full = grad_middle + norm_backward(
        grad_normed_one, normed_one, scale_one, attn_set[0].astype(jnp.float32)
    )
    input_grad = input_full.astype(jnp.bfloat16).reshape(row_count, length, width)
    attn_parts = (
        lax.psum_scatter(gain_one_grad, "fsdp", scatter_dimension=0, tiled=True),
        lax.psum_scatter(query_grad, "fsdp", scatter_dimension=0, tiled=True),
        lax.psum_scatter(key_grad, "fsdp", scatter_dimension=0, tiled=True),
        lax.psum_scatter(value_grad, "fsdp", scatter_dimension=0, tiled=True),
        lax.psum_scatter(out_grad, "fsdp", scatter_dimension=0, tiled=True),
    )
    every = attn_parts + ffn_parts
    return (
        output,
        input_grad,
        every[0],
        every[1],
        every[2],
        every[3],
        every[4],
        every[5],
        every[6],
        every[7],
        every[8],
    )


def solution(mesh):
    placed = (
        P("fsdp", None, None),
        P("fsdp", None),
        P("fsdp"),
        P("fsdp", None),
        P("fsdp", None),
        P("fsdp", None),
        P("fsdp", None),
        P("fsdp"),
        P("fsdp", None),
        P("fsdp", None),
        P("fsdp", None),
        P("fsdp", None, None),
    )
    return jax.shard_map(
        per_device,
        mesh=mesh,
        in_specs=placed,
        out_specs=(
            P("fsdp", None, None),
            P("fsdp", None, None),
            P("fsdp"),
            P("fsdp", None),
            P("fsdp", None),
            P("fsdp", None),
            P("fsdp", None),
            P("fsdp"),
            P("fsdp", None),
            P("fsdp", None),
            P("fsdp", None),
        ),
        check_vma=False,
    )
```

profile of v0, /device:TPU:0, one launch (start us, length us, event | category | flops | bytes accessed | tf_op | source)
XLA Modules:
  0.0 1243.9 jit_solution(14992071916210314030)
XLA Ops:
  13.9 42.1 %all-reduce.5 = (bf16[768]{0:T(1024)(128)(2,1)S(1)}, bf16[768]{0:T(1024)(128)(2,1)S(1)}) all-reduce(bf16[768]{0:T(1024)(128)(2,1)S(1)} %dynamic-update-slice, bf16[768]{0:T(1024)(128)(2,1)S(1)} %dynamic-update-slice.1), channel_id=1, replica_groups=mesh['fsdp'=32] {'fsdp'}, use_global_device_ids=true, to_apply=%add | all-reduce | flops 1536 | bytes 6144
  58.2 9.6 all-gather.10.cloned.1.call-done
  67.7 2.4 copy.54
  70.1 53.5 %all-gather.8.cloned.1.call-done = bf16[768,768]{1,0:T(8,128)(2,1)} async-done(((bf16[24,768]{1,0:T(8,128)(2,1)}), bf16[768,768]{1,0:T(8,128)(2,1)}) %all-gather.8.cloned.1.call-update) | async-done | bytes 1179664 | tf_op jit(solution)/shard_map/all_gather | solution.py:109
  125.2 2.8 convolution_bitcast_fusion
  131.6 3.9 copy.56
  135.6 2.6 copy.57
  138.1 41.4 %all-gather.12.cloned.1.call-done = bf16[768,768]{1,0:T(8,128)(2,1)} async-done(((bf16[24,768]{1,0:T(8,128)(2,1)}), bf16[768,768]{1,0:T(8,128)(2,1)}) %all-gather.12.cloned.1.call-update) | async-done | bytes 1179664 | tf_op jit(solution)/shard_map/all_gather | solution.py:111
  179.5 2.4 convolution_convert_fusion.1
  182.8 2.5 copy.58
  185.3 54.6 %while.50 = (s32[]{:T(128)}, bf16[12,784,64]{1,2,0:T(8,128)(2,1)}, f32[12,784]{1,0:T(8,128)S(1)}, bf16[12,784,64]{2,1,0:T(8,128)(2,1)}, bf16[12,784,64]{2,1,0:T(...) while((s32[]{:T(128)}, bf16[12,784,64]{1,2,0:T(8,128)(2,1)}, ...), condition=%wide.region_6.7_spmd.clone.clone, body=%wide.region_3.6_spmd.clone.sunk.clone | while | flops 164112368 | bytes 8255313 | solution.py:153
  187.7 2.2 fusion.169
  192.2 2.2 fusion.169
  196.8 2.2 fusion.169
  201.3 2.2 fusion.169
  205.9 2.2 fusion.169
  210.4 2.2 fusion.169
  215.0 2.2 fusion.169
  219.5 2.2 fusion.169
  224.0 2.2 fusion.169
  228.6 2.2 fusion.169
  233.1 2.2 fusion.169
  237.7 2.2 fusion.169
  239.9 3.4 multiply_reduce_fusion.3
  245.1 50.8 %all-gather.16.cloned.1.call-done = bf16[768,2048]{1,0:T(8,128)(2,1)} async-done(((bf16[24,2048]{1,0:T(8,128)(2,1)}), bf16[768,2048]{1,0:T(8,128)(2,1)}) %all-gather.16.cloned.1.call-update) | async-done | bytes 3145744 | tf_op jit(solution)/shard_map/all_gather | solution.py:116
  295.9 6.4 fusion.95
  302.3 54.1 %all-gather.18.cloned.1.call-done = bf16[768,2048]{1,0:T(8,128)(2,1)} async-done(((bf16[24,2048]{1,0:T(8,128)(2,1)}), bf16[768,2048]{1,0:T(8,128)(2,1)}) %all-gather.18.cloned.1.call-update) | async-done | bytes 3145744 | tf_op jit(solution)/shard_map/all_gather | solution.py:117
  356.4 6.8 fusion.96
  363.2 53.8 %all-gather.20.cloned.1.call-done = bf16[2048,768]{1,0:T(8,128)(2,1)} async-done(((bf16[64,768]{1,0:T(8,128)(2,1)}), bf16[2048,768]{1,0:T(8,128)(2,1)}) %all-gather.20.cloned.1.call-update) | async-done | bytes 3145744 | tf_op jit(solution)/shard_map/all_gather | solution.py:118
  417.0 9.8 multiply_convert_fusion.1
  426.9 2.7 fusion.97
  431.8 3.1 multiply_reduce_fusion.1
  437.1 2.8 fusion.85
  439.9 3.8 convolution_convert_fusion
  443.8 2.7 copy.59
  446.5 114.9 %while.51 = (s32[]{:T(128)}, f32[12,784,64]{1,2,0:T(8,128)}, f32[12,784,64]{1,2,0:T(8,128)}, bf16[12,784,64]{1,2,0:T(8,128)(2,1)S(1)}, bf16[12,784,64]{2,1,0:T(8...) while((s32[]{:T(128)}, f32[12,784,64]{1,2,0:T(8,128)}, ...), condition=%wide.region_11.12_spmd.clone.clone, body=%wide.region_9.11_spmd.clone.sunk.clone | while | flops 400855296 | bytes 20741992 | solution.py:215
  450.4 2.2 fusion.179
  460.0 2.2 fusion.179
  469.6 2.2 fusion.179
  479.2 2.2 fusion.179
  488.8 2.2 fusion.179
  498.4 2.2 fusion.179
  507.9 2.2 fusion.179
  517.5 2.2 fusion.179
  527.0 2.2 fusion.179
  555.7 2.2 fusion.179
  561.4 4.2 multiply_add_fusion.1
  567.2 3.1 fusion.81
  573.0 3.1 fusion.77
  576.2 4.4 fusion.79
  580.7 7.3 fusion.100
  588.0 7.3 fusion.101
  596.6 8.0 fusion.71
  606.0 2.8 fusion.99
  610.5 3.3 fusion.64
  613.8 38.6 %all-reduce.4 = (f32[768]{0:T(1024)S(1)}, f32[768]{0:T(1024)S(1)}) all-reduce(f32[768]{0:T(1024)S(1)} %get-tuple-element.269, f32[768]{0:T(1024)S(1)} %get-tuple-element.267), channel_id=2, replica_groups=mesh['fsdp'=32] {'fsdp'}, use_global_device_ids=true, to_apply=%region_14.15.clone | all-reduce | flops 1536 | bytes 12288
  653.5 4.3 fusion.69
  657.8 5.6 fusion.68
  663.4 5.0 reduce-scatter.10.cloned.1.call-done
  668.4 103.8 %reduce-scatter.8.cloned.1.call-done = f32[24,768]{1,0:T(8,128)} async-done(((f32[768,768]{1,0:T(8,128)}), f32[24,768]{1,0:T(8,128)}) %reduce-scatter.8.cloned.1.call-update) | async-done | bytes 73744 | tf_op jit(solution)/shard_map/reduce_scatter | solution.py:256
  772.2 104.7 %reduce-scatter.12.cloned.1.call-done = f32[24,768]{1,0:T(8,128)} async-done(((f32[768,768]{1,0:T(8,128)}), f32[24,768]{1,0:T(8,128)}) %reduce-scatter.12.cloned.1.call-update) | async-done | bytes 73744 | tf_op jit(solution)/shard_map/reduce_scatter | solution.py:258
  876.9 119.7 %reduce-scatter.16.cloned.1.call-done = f32[24,2048]{1,0:T(8,128)} async-done(((f32[768,2048]{1,0:T(8,128)}), f32[24,2048]{1,0:T(8,128)}) %reduce-scatter.16.cloned.1.call-update) | async-done | bytes 196624 | tf_op jit(solution)/shard_map/reduce_scatter | solution.py:190
  996.6 120.9 %reduce-scatter.18.cloned.1.call-done = f32[24,2048]{1,0:T(8,128)} async-done(((f32[768,2048]{1,0:T(8,128)}), f32[24,2048]{1,0:T(8,128)}) %reduce-scatter.18.cloned.1.call-update) | async-done | bytes 196624 | tf_op jit(solution)/shard_map/reduce_scatter | solution.py:191
  1117.5 119.6 %reduce-scatter.20.cloned.1.call-done = f32[64,768]{1,0:T(8,128)} async-done(((f32[2048,768]{1,0:T(8,128)}), f32[64,768]{1,0:T(8,128)}) %reduce-scatter.20.cloned.1.call-update) | async-done | bytes 196624 | tf_op jit(solution)/shard_map/reduce_scatter | solution.py:192
  (250 shorter events, 150.7 us)
Async XLA Ops:
  7.2 48.8 %copy-start.2 = (bf16[1,784,768]{2,1,0:T(8,128)(2,1)S(1)}, bf16[1,784,768]{2,1,0:T(8,128)(2,1)}, u32[]{:S(2)}) copy-start(bf16[1,784,768]{2,1,0:T(8,128)(2,1)} %param.16) | copy-start | bytes 3612676
  7.2 49.1 %copy-start.21 = (s32[1,784]{1,0:T(1,128)S(1)}, s32[1,784]{1,0:T(1,128)}, u32[]{:S(2)}) copy-start(s32[1,784]{1,0:T(1,128)} %param.17) | copy-start | bytes 9412
  7.2 60.5 %all-gather.10.cloned.1.call-start = ((), (), s32[]{:S(2)}) async-start(), calls=%async_computation.8 | async-start | bytes 1216512 | tf_op jit(solution)/shard_map/all_gather | solution.py:110
  7.9 115.7 %all-gather.8.cloned.1.call-start = ((), (), s32[]{:S(2)}) async-start(), calls=%async_computation.7 | async-start | bytes 1216512 | tf_op jit(solution)/shard_map/all_gather | solution.py:109
  8.7 170.8 %all-gather.12.cloned.1.call-start = ((), (), s32[]{:S(2)}) async-start(), calls=%async_computation.9 | async-start | bytes 1216512 | tf_op jit(solution)/shard_map/all_gather | solution.py:111
  9.4 230.5 %all-gather.14.cloned.1.call-start = ((), (), s32[]{:S(2)}) async-start(), calls=%async_computation.10 | async-start | bytes 1216512 | tf_op jit(solution)/shard_map/all_gather | solution.py:112
  10.0 285.9 %all-gather.16.cloned.1.call-start = ((), (), s32[]{:S(2)}) async-start(), calls=%async_computation.11 | async-start | bytes 3244032 | tf_op jit(solution)/shard_map/all_gather | solution.py:116
  10.6 345.8 %all-gather.18.cloned.1.call-start = ((), (), s32[]{:S(2)}) async-start(), calls=%async_computation.12 | async-start | bytes 3244032 | tf_op jit(solution)/shard_map/all_gather | solution.py:117
  11.2 405.9 %all-gather.20.cloned.1.call-start = ((), (), s32[]{:S(2)}) async-start(), calls=%async_computation.13 | async-start | bytes 3244032 | tf_op jit(solution)/shard_map/all_gather | solution.py:118
  11.9 651.5 %reduce-scatter.14.cloned.1.call-start = ((), (), s32[]{:S(2)}) async-start(), calls=%async_computation.17 | async-start | bytes 2433024 | tf_op jit(solution)/shard_map/reduce_scatter | solution.py:259
  12.2 58.0 %copy-start = (bf16[12,784,64]{1,2,0:T(8,128)(2,1)}, bf16[12,784,64]{1,2,0:T(8,128)(2,1)S(1)}, u32[]{:S(2)}) copy-start(bf16[12,784,64]{1,2,0:T(8,128)(2,1)S(1)} %fusion.94) | copy-start | bytes 3612676
  243.3 1.5 copy-start.6
  302.3 114.8 %copy-start.17 = (bf16[1,784,768]{2,1,0:T(8,128)(2,1)S(1)}, bf16[1,784,768]{2,1,0:T(8,128)(2,1)}, u32[]{:S(2)}) copy-start(bf16[1,784,768]{2,1,0:T(8,128)(2,1)} %param.27) | copy-start | bytes 3612676
  417.0 9.8 copy-start.23
  426.8 2.7 copy-start.11
  426.8 3.3 copy-start.10
  426.9 3.5 copy-start.7
  426.9 4.9 copy-start.24
  434.9 2.1 copy-start.16
  435.6 1.4 copy-start.9
  437.1 2.9 copy-start.25
  439.9 228.5 %reduce-scatter.10.cloned.1.call-start = ((), (), s32[]{:S(2)}) async-start(), calls=%async_computation.15 | async-start | bytes 2433024 | tf_op jit(solution)/shard_map/reduce_scatter | solution.py:257
  443.8 2.8 copy-start.1
  565.6 1.6 copy-start.3
  565.9 1.1 copy-start.12
  570.4 201.8 %reduce-scatter.8.cloned.1.call-start = ((), (), s32[]{:S(2)}) async-start(), calls=%async_computation.14 | async-start | bytes 2433024 | tf_op jit(solution)/shard_map/reduce_scatter | solution.py:256
  570.5 2.5 copy-start.4
  571.9 1.1 copy-start.14
  576.1 300.8 %reduce-scatter.12.cloned.1.call-start = ((), (), s32[]{:S(2)}) async-start(), calls=%async_computation.16 | async-start | bytes 2433024 | tf_op jit(solution)/shard_map/reduce_scatter | solution.py:258
  580.6 415.9 %reduce-scatter.16.cloned.1.call-start = ((), (), s32[]{:S(2)}) async-start(), calls=%async_computation.18 | async-start | bytes 6488064 | tf_op jit(solution)/shard_map/reduce_scatter | solution.py:190
  588.0 529.5 %reduce-scatter.18.cloned.1.call-start = ((), (), s32[]{:S(2)}) async-start(), calls=%async_computation.19 | async-start | bytes 6488064 | tf_op jit(solution)/shard_map/reduce_scatter | solution.py:191
  595.3 1.3 copy-start.18
  595.3 641.8 %reduce-scatter.20.cloned.1.call-start = ((), (), s32[]{:S(2)}) async-start(), calls=%async_computation.20 | async-start | bytes 6488064 | tf_op jit(solution)/shard_map/reduce_scatter | solution.py:192
  604.7 1.4 copy-start.13
  606.0 2.8 copy-start.15
  606.0 2.8 copy-start.20
  608.8 1.4 copy-start.5
  608.8 1.6 copy-start.19
  653.5 4.3 copy-start.8
  653.5 4.3 copy-start.22
Sparse Core Ops, SparseCore 0:
  10.9 56.7 all-gather.9
  70.6 52.9 all-gather.7
  126.5 52.9 all-gather.11
  182.3 52.9 all-gather.13
  238.0 57.8 all-gather.15
  298.6 57.7 all-gather.17
  359.3 57.7 all-gather.19
  440.0 97.8 reduce-scatter.13
  570.5 97.8 reduce-scatter.9
  674.1 98.0 reduce-scatter.7
  779.0 97.8 reduce-scatter.11
  883.0 113.5 reduce-scatter.15
  1003.7 113.7 reduce-scatter.17
  1123.5 113.5 reduce-scatter.19
where the time goes:
time: 1260 us; the launch traced here: 1240 us
  waiting for transfers between devices  841 us (67%)
  matrix products  248 us (20%)
  blocking collectives  80.7 us (6%)
  local copies, waits for them, and re-layouts  32.2 us (3%)
  other arithmetic  25.2 us (2%)
  between operations  14.5 us (1%)
    reduce_scatter x1, waiting for transfers between devices, per_device(): lax.psum_scatter(up_grad, 'fsdp', scatter_dimension=0, tiled=True)  121 us
    reduce_scatter x1, waiting for transfers between devices, per_device(): lax.psum_scatter(gate_grad, 'fsdp', scatter_dimension=0, tiled=True)  120 us
    reduce_scatter x1, waiting for transfers between devices, per_device(): lax.psum_scatter(down_grad, 'fsdp', scatter_dimension=0, tiled=True)  120 us
    reduce_scatter x1, waiting for transfers between devices, per_device(): lax.psum_scatter(value_grad, 'fsdp', scatter_dimension=0, tiled=True)  105 us
    reduce_scatter x1, waiting for transfers between devices, per_device(): lax.psum_scatter(query_grad, 'fsdp', scatter_dimension=0, tiled=True)  104 us
    unnamed x2, blocking collectives  80.7 us
    all_gather x1, waiting for transfers between devices, per_device(): lax.all_gather(w_up, 'fsdp', axis=0, tiled=True)  54.1 us
    all_gather x1, waiting for transfers between devices, per_device(): lax.all_gather(w_down, 'fsdp', axis=0, tiled=True)  53.8 us
  transfers between devices with their start and end apart: 14, of which 12 were waited for; matrix products, arithmetic and copies ran while one was open for 22% of the time, Pallas kernels for 0%

commit v1 on v0

--- a/solution.py
+++ b/solution.py
@@ -6,6 +6,18 @@
 
 HEAD = 64
 EPSILON = 1e-05
+
+
+def gather_by_bits(value, axis, dim):
+    ways, here, step = (lax.axis_size(axis), lax.axis_index(axis), value.shape[dim])
+    line, have = (value, 1)
+    while have < ways:
+        line = jnp.concatenate(
+            [line, lax.ppermute(line, axis, [(d, (d - have) % ways) for d in range(ways)])],
+            axis=dim,
+        )
+        have = 2 * have
+    return jnp.roll(line, here * step, axis=dim)
 
 
 def rope_tables(segment_row, head_size):
@@ -108,7 +120,7 @@
         lax.all_gather(gain_attn, "fsdp", axis=0, tiled=True),
         lax.all_gather(w_query, "fsdp", axis=0, tiled=True),
         lax.all_gather(w_key, "fsdp", axis=0, tiled=True),
-        lax.all_gather(w_value, "fsdp", axis=0, tiled=True),
+        gather_by_bits(w_value, "fsdp", 0),
         lax.all_gather(w_out, "fsdp", axis=0, tiled=True),
     )
     ffn_set = (

time: 1260 us -> 1220 us (0.968)
  waiting for transfers between devices: 841 us -> 746 us
  local copies, waits for them, and re-layouts: 32.2 us -> 65.7 us
  blocking collectives: 80.7 us -> 94.1 us
    all_gather x1 -> x0, waiting for transfers between devices: 41.4 us -> none  [per_device(): lax.all_gather(w_value, 'fsdp', axis=0, tiled=True)]
    all_gather x1, waiting for transfers between devices: 53.5 us -> 16.2 us  [per_device(): lax.all_gather(w_query, 'fsdp', axis=0, tiled=True)]
    all_gather x1, waiting for transfers between devices: 54.1 us -> 32 us  [per_device(): lax.all_gather(w_up, 'fsdp', axis=0, tiled=True)]
    dynamic_update_slice x12, local copies, waits for them, and re-layouts: 1.19 us -> 16.6 us  [row_forward(): return lax.map(one_head, (query_row, key_row, value_row))]
    ppermute x0 -> x5, waiting for transfers between devices: none -> 13.6 us  [gather_by_bits(): lax.ppermute(line, axis, [(d, (d - have) % ways) for d in range(ways)])]
    unnamed x2, blocking collectives: 80.7 us -> 94.1 us
    unnamed x62 -> x88, local copies, waits for them, and re-layouts: 23.2 us -> 30.4 us
  transfers between devices with their start and end apart: 14 -> 18, of which waited for: 12 -> 13; matrix products, arithmetic and copies ran while one was open for 22% -> 26% of each run, Pallas kernels for 0% -> 0%
where the time goes in v1:
time: 1220 us; the launch traced here: 1210 us
  waiting for transfers between devices  746 us (61%)
  matrix products  250 us (20%)
  blocking collectives  94.1 us (8%)
  local copies, waits for them, and re-layouts  65.7 us (5%)
  other arithmetic  29.7 us (2%)
  between operations  14.6 us (1%)
    reduce_scatter x1, waiting for transfers between devices, per_device(): lax.psum_scatter(gate_grad, 'fsdp', scatter_dimension=0, tiled=True)  121 us
    reduce_scatter x1, waiting for transfers between devices, per_device(): lax.psum_scatter(down_grad, 'fsdp', scatter_dimension=0, tiled=True)  120 us
    reduce_scatter x1, waiting for transfers between devices, per_device(): lax.psum_scatter(up_grad, 'fsdp', scatter_dimension=0, tiled=True)  120 us
    reduce_scatter x1, waiting for transfers between devices, per_device(): lax.psum_scatter(value_grad, 'fsdp', scatter_dimension=0, tiled=True)  105 us
    reduce_scatter x1, waiting for transfers between devices, per_device(): lax.psum_scatter(query_grad, 'fsdp', scatter_dimension=0, tiled=True)  104 us
    unnamed x2, blocking collectives  94.1 us
    all_gather x1, waiting for transfers between devices, per_device(): lax.all_gather(w_gate, 'fsdp', axis=0, tiled=True)  54.1 us
    all_gather x1, waiting for transfers between devices, per_device(): lax.all_gather(w_down, 'fsdp', axis=0, tiled=True)  53.6 us
  transfers between devices with their start and end apart: 18, of which 13 were waited for; matrix products, arithmetic and copies ran while one was open for 26% of the time, Pallas kernels for 0%

profile of v1, /device:TPU:0, one launch (start us, length us, event | category | flops | bytes accessed | tf_op | source)
XLA Modules:
  0.0 1210.8 jit_solution(6549738125295511537)
XLA Ops:
  10.6 6.4 collective-permute-start
  26.3 5.0 collective-permute-done.2
  34.5 6.7 collective-permute-done.3
  43.2 55.4 %all-reduce.5 = (bf16[768]{0:T(1024)(128)(2,1)S(1)}, bf16[768]{0:T(1024)(128)(2,1)S(1)}) all-reduce(bf16[768]{0:T(1024)(128)(2,1)S(1)} %dynamic-update-slice, bf16[768]{0:T(1024)(128)(2,1)S(1)} %dynamic-update-slice.1), channel_id=1, replica_groups=mesh['fsdp'=32] {'fsdp'}, use_global_device_ids=true, to_apply=%add | all-reduce | flops 1536 | bytes 6144
  108.3 3.5 convolution_convert_fusion.1
  113.6 2.5 copy.58
  117.7 3.0 convolution_bitcast_fusion
  120.7 16.2 %all-gather.7.cloned.1.call-done = bf16[768,768]{1,0:T(8,128)(2,1)} async-done(((bf16[24,768]{1,0:T(8,128)(2,1)}), bf16[768,768]{1,0:T(8,128)(2,1)}) %all-gather.7.cloned.1.call-update) | async-done | bytes 1179664 | tf_op jit(solution)/shard_map/all_gather | solution.py:121
  141.5 2.5 copy.56
  144.0 2.6 copy.57
  146.6 69.8 %while.50 = (s32[]{:T(128)}, bf16[12,784,64]{1,2,0:T(8,128)(2,1)}, f32[12,784]{1,0:T(8,128)}, bf16[12,784,64]{2,1,0:T(8,128)(2,1)}, bf16[12,784,64]{2,1,0:T(8,12...) while((s32[]{:T(128)}, bf16[12,784,64]{1,2,0:T(8,128)(2,1)}, ...), condition=%wide.region_6.7_spmd.clone.clone, body=%wide.region_3.6_spmd.clone.sunk.clone | while | flops 164112368 | bytes 8255313 | solution.py:165
  150.2 2.2 fusion.171
  156.0 2.2 fusion.171
  161.9 2.2 fusion.171
  167.7 2.2 fusion.171
  173.5 2.2 fusion.171
  179.3 2.2 fusion.171
  185.1 2.2 fusion.171
  190.9 2.2 fusion.171
  196.7 2.2 fusion.171
  202.5 2.2 fusion.171
  208.4 2.2 fusion.171
  214.2 2.2 fusion.171
  216.4 3.4 multiply_reduce_fusion.3
  221.5 32.0 %all-gather.15.cloned.1.call-done = bf16[768,2048]{1,0:T(8,128)(2,1)} async-done(((bf16[24,2048]{1,0:T(8,128)(2,1)}), bf16[768,2048]{1,0:T(8,128)(2,1)}) %all-gather.15.cloned.1.call-update) | async-done | bytes 3145744 | tf_op jit(solution)/shard_map/all_gather | solution.py:129
  253.5 6.4 fusion.100
  259.9 54.1 %all-gather.13.cloned.1.call-done = bf16[768,2048]{1,0:T(8,128)(2,1)} async-done(((bf16[24,2048]{1,0:T(8,128)(2,1)}), bf16[768,2048]{1,0:T(8,128)(2,1)}) %all-gather.13.cloned.1.call-update) | async-done | bytes 3145744 | tf_op jit(solution)/shard_map/all_gather | solution.py:128
  314.0 6.9 fusion.99
  320.9 53.6 %all-gather.17.cloned.1.call-done = bf16[2048,768]{1,0:T(8,128)(2,1)} async-done(((bf16[64,768]{1,0:T(8,128)(2,1)}), bf16[2048,768]{1,0:T(8,128)(2,1)}) %all-gather.17.cloned.1.call-update) | async-done | bytes 3145744 | tf_op jit(solution)/shard_map/all_gather | solution.py:130
  374.5 9.8 multiply_convert_fusion.1
  384.4 2.7 fusion.101
  389.3 3.1 multiply_reduce_fusion.1
  394.6 2.9 fusion.87
  397.5 3.8 convolution_convert_fusion
  401.4 2.7 copy.59
  404.1 123.8 %while.51 = (s32[]{:T(128)}, f32[12,784,64]{1,2,0:T(8,128)}, f32[12,784,64]{1,2,0:T(8,128)}, bf16[12,784,64]{1,2,0:T(8,128)(2,1)S(1)}, bf16[12,784,64]{2,1,0:T(8...) while((s32[]{:T(128)}, f32[12,784,64]{1,2,0:T(8,128)}, ...), condition=%wide.region_11.12_spmd.clone.clone, body=%wide.region_9.11_spmd.clone.sunk.clone | while | flops 400855296 | bytes 20741992 | solution.py:227
  408.7 2.2 fusion.181
  419.0 2.2 fusion.181
  429.4 2.2 fusion.181
  450.0 2.2 fusion.181
  460.4 2.2 fusion.181
  470.6 2.2 fusion.181
  481.0 2.2 fusion.181
  491.3 2.2 fusion.181
  501.6 2.2 fusion.181
  511.9 2.2 fusion.181
  527.9 4.2 multiply_add_fusion.1
  533.7 3.2 fusion.81
  539.5 3.1 fusion.77
  542.7 4.4 fusion.79
  547.2 7.3 fusion.105
  554.5 7.3 fusion.104
  563.1 8.1 fusion.71
  572.6 2.8 fusion.103
  577.5 3.3 fusion.64
  580.8 38.7 %all-reduce.4 = (f32[768]{0:T(1024)S(1)}, f32[768]{0:T(1024)S(1)}) all-reduce(f32[768]{0:T(1024)S(1)} %get-tuple-element.269, f32[768]{0:T(1024)S(1)} %get-tuple-element.267), channel_id=2, replica_groups=mesh['fsdp'=32] {'fsdp'}, use_global_device_ids=true, to_apply=%region_14.15.clone | all-reduce | flops 1536 | bytes 12288
  620.7 4.3 fusion.69
  624.9 5.6 fusion.68
  630.5 4.6 reduce-scatter.10.cloned.1.call-done
  635.1 103.9 %reduce-scatter.8.cloned.1.call-done = f32[24,768]{1,0:T(8,128)} async-done(((f32[768,768]{1,0:T(8,128)}), f32[24,768]{1,0:T(8,128)}) %reduce-scatter.8.cloned.1.call-update) | async-done | bytes 73744 | tf_op jit(solution)/shard_map/reduce_scatter | solution.py:268
  739.0 104.6 %reduce-scatter.12.cloned.1.call-done = f32[24,768]{1,0:T(8,128)} async-done(((f32[768,768]{1,0:T(8,128)}), f32[24,768]{1,0:T(8,128)}) %reduce-scatter.12.cloned.1.call-update) | async-done | bytes 73744 | tf_op jit(solution)/shard_map/reduce_scatter | solution.py:270
  843.6 119.8 %reduce-scatter.18.cloned.1.call-done = f32[24,2048]{1,0:T(8,128)} async-done(((f32[768,2048]{1,0:T(8,128)}), f32[24,2048]{1,0:T(8,128)}) %reduce-scatter.18.cloned.1.call-update) | async-done | bytes 196624 | tf_op jit(solution)/shard_map/reduce_scatter | solution.py:203
  963.4 120.7 %reduce-scatter.16.cloned.1.call-done = f32[24,2048]{1,0:T(8,128)} async-done(((f32[768,2048]{1,0:T(8,128)}), f32[24,2048]{1,0:T(8,128)}) %reduce-scatter.16.cloned.1.call-update) | async-done | bytes 196624 | tf_op jit(solution)/shard_map/reduce_scatter | solution.py:202
  1084.1 119.9 %reduce-scatter.20.cloned.1.call-done = f32[64,768]{1,0:T(8,128)} async-done(((f32[2048,768]{1,0:T(8,128)}), f32[64,768]{1,0:T(8,128)}) %reduce-scatter.20.cloned.1.call-update) | async-done | bytes 196624 | tf_op jit(solution)/shard_map/reduce_scatter | solution.py:204
  (288 shorter events, 196.0 us)
Async XLA Ops:
  7.2 24.1 %copy-start.23 = (bf16[24,768]{1,0:T(8,128)(2,1)S(1)}, bf16[24,768]{1,0:T(8,128)(2,1)}, u32[]{:S(2)}) copy-start(bf16[24,768]{1,0:T(8,128)(2,1)} %param.21) | copy-start | bytes 110596
  7.2 109.0 %all-gather.9.cloned.1.call-start = ((), (), s32[]{:S(2)}) async-start(), calls=%async_computation.8 | async-start | bytes 1216512 | tf_op jit(solution)/shard_map/all_gather | solution.py:122
  7.9 129.0 %all-gather.7.cloned.1.call-start = ((), (), s32[]{:S(2)}) async-start(), calls=%async_computation.7 | async-start | bytes 1216512 | tf_op jit(solution)/shard_map/all_gather | solution.py:121
  8.7 207.7 %all-gather.11.cloned.1.call-start = ((), (), s32[]{:S(2)}) async-start(), calls=%async_computation.9 | async-start | bytes 1216512 | tf_op jit(solution)/shard_map/all_gather | solution.py:124
  9.4 244.1 %all-gather.15.cloned.1.call-start = ((), (), s32[]{:S(2)}) async-start(), calls=%async_computation.11 | async-start | bytes 3244032 | tf_op jit(solution)/shard_map/all_gather | solution.py:129
  10.0 304.0 %all-gather.13.cloned.1.call-start = ((), (), s32[]{:S(2)}) async-start(), calls=%async_computation.10 | async-start | bytes 3244032 | tf_op jit(solution)/shard_map/all_gather | solution.py:128
  10.6 363.9 %all-gather.17.cloned.1.call-start = ((), (), s32[]{:S(2)}) async-start(), calls=%async_computation.12 | async-start | bytes 3244032 | tf_op jit(solution)/shard_map/all_gather | solution.py:130
  10.6 8.9 collective-permute-start
  17.1 613.5 %reduce-scatter.14.cloned.1.call-start = ((), (), s32[]{:S(2)}) async-start(), calls=%async_computation.16 | async-start | bytes 2433024 | tf_op jit(solution)/shard_map/reduce_scatter | solution.py:271
  18.7 24.0 %copy-start.32 = (bf16[24]{0:T(256)(128)(2,1)S(1)}, bf16[24]{0:T(256)(128)(2,1)}, u32[]{:S(2)}) copy-start(bf16[24]{0:T(256)(128)(2,1)} %param.18) | copy-start | bytes 148
  18.7 24.2 %copy-start.33 = (bf16[24]{0:T(256)(128)(2,1)S(1)}, bf16[24]{0:T(256)(128)(2,1)}, u32[]{:S(2)}) copy-start(bf16[24]{0:T(256)(128)(2,1)} %param.23) | copy-start | bytes 148
  19.5 80.2 %copy-start.26 = (s32[784]{0:T(1024)}, s32[784]{0:T(1024)S(1)}, u32[]{:S(2)}) copy-start(s32[784]{0:T(1024)S(1)} %reduce.3) | copy-start | bytes 9412
  19.5 80.2 %copy-start.24 = (bf16[24,768]{1,0:T(8,128)(2,1)}, bf16[24,768]{1,0:T(8,128)(2,1)S(1)}, u32[]{:S(2)}) copy-start(bf16[24,768]{1,0:T(8,128)(2,1)S(1)} %collective-permute-done) | copy-start | bytes 110596
  20.3 4.4 collective-permute-start.1
  25.4 5.8 collective-permute-start.2
  26.3 73.3 %copy-start = (bf16[12,784,64]{1,2,0:T(8,128)(2,1)}, bf16[12,784,64]{1,2,0:T(8,128)(2,1)S(1)}, u32[]{:S(2)}) copy-start(bf16[12,784,64]{1,2,0:T(8,128)(2,1)S(1)} %fusion.98) | copy-start | bytes 3612676
  31.3 10.0 collective-permute-start.3
  41.3 57.3 %copy-start.20 = (bf16[192,768]{1,0:T(8,128)(2,1)}, bf16[192,768]{1,0:T(8,128)(2,1)S(1)}, u32[]{:S(2)}) copy-start(bf16[192,768]{1,0:T(8,128)(2,1)S(1)} %collective-permute-done.3) | copy-start | bytes 884740
  42.2 59.4 %collective-permute-start.4 = (bf16[384,768]{1,0:T(8,128)(2,1)}, bf16[384,768]{1,0:T(8,128)(2,1)S(1)}, u32[]{:S(2)}, u32[]{:S(2)}) collective-permute-start(bf16[384,768]{1,0:T(8,128)(2,1)} %get-tuple-element.326), channel_id=1, source_target_pairs={{0,16},{1,17},{2,18},{3,19},{4,20},{5,21},{6,22},{7,23},{8,24},{9,... | collective-permute-start | bytes 1769480 | tf_op jit(solution)/shard_map/ppermute | solution.py:16
  99.6 8.7 copy-start.2
  138.5 1.8 copy-start.12
  138.5 1.8 copy-start.22
  144.0 2.6 copy-start.27
  219.8 1.4 copy-start.6
  259.9 114.6 %copy-start.18 = (bf16[1,784,768]{2,1,0:T(8,128)(2,1)S(1)}, bf16[1,784,768]{2,1,0:T(8,128)(2,1)}, u32[]{:S(2)}) copy-start(bf16[1,784,768]{2,1,0:T(8,128)(2,1)} %param.27) | copy-start | bytes 3612676
  374.5 9.9 copy-start.30
  384.3 2.7 copy-start.10
  384.3 3.3 copy-start.11
  384.3 3.5 copy-start.7
  384.4 4.9 copy-start.29
  392.4 2.2 copy-start.15
  393.1 1.5 copy-start.9
  394.6 2.9 copy-start.31
  397.5 237.6 %reduce-scatter.10.cloned.1.call-start = ((), (), s32[]{:S(2)}) async-start(), calls=%async_computation.14 | async-start | bytes 2433024 | tf_op jit(solution)/shard_map/reduce_scatter | solution.py:269
  401.4 2.7 copy-start.1
  532.2 1.6 copy-start.3
  532.4 1.1 copy-start.13
  536.9 202.0 %reduce-scatter.8.cloned.1.call-start = ((), (), s32[]{:S(2)}) async-start(), calls=%async_computation.13 | async-start | bytes 2433024 | tf_op jit(solution)/shard_map/reduce_scatter | solution.py:268
  537.0 2.5 copy-start.4
  538.4 1.1 copy-start.16
  542.6 301.0 %reduce-scatter.12.cloned.1.call-start = ((), (), s32[]{:S(2)}) async-start(), calls=%async_computation.15 | async-start | bytes 2433024 | tf_op jit(solution)/shard_map/reduce_scatter | solution.py:270
  547.1 416.2 %reduce-scatter.18.cloned.1.call-start = ((), (), s32[]{:S(2)}) async-start(), calls=%async_computation.18 | async-start | bytes 6488064 | tf_op jit(solution)/shard_map/reduce_scatter | solution.py:203
  554.5 529.6 %reduce-scatter.16.cloned.1.call-start = ((), (), s32[]{:S(2)}) async-start(), calls=%async_computation.17 | async-start | bytes 6488064 | tf_op jit(solution)/shard_map/reduce_scatter | solution.py:202
  561.8 1.3 copy-start.19
  561.9 642.2 %reduce-scatter.20.cloned.1.call-start = ((), (), s32[]{:S(2)}) async-start(), calls=%async_computation.19 | async-start | bytes 6488064 | tf_op jit(solution)/shard_map/reduce_scatter | solution.py:204
  571.3 1.4 copy-start.14
  572.6 2.8 copy-start.17
  572.6 2.8 copy-start.21
  575.4 1.4 copy-start.5
  575.4 2.0 copy-start.25
  620.7 4.3 copy-start.8
  620.7 4.3 copy-start.28
Sparse Core Ops, SparseCore 0:
  10.9 69.2 all-gather.8
  83.1 53.7 all-gather.6
  139.8 52.9 all-gather.10
  195.6 57.8 all-gather.14
  256.2 57.7 all-gather.12
  316.7 57.7 all-gather.16
  397.6 97.8 reduce-scatter.13
  537.1 97.9 reduce-scatter.9
  641.0 97.9 reduce-scatter.7
  745.5 98.0 reduce-scatter.11
  849.8 113.4 reduce-scatter.17
  970.4 113.6 reduce-scatter.15
  1090.3 113.6 reduce-scatter.19
